TPU v7x, 32 devices: a whole 2x2x4 slice. The times are simulated.
32 devices in a mesh: cores: 4 (over y, x), mode: 8 (over z, core).
Axes of the slice: x: 2, y: 2, z: 4, core: 2. Of those that a mesh axis runs over, the one named last changes fastest.
Arguments:
- x_cores: bfloat16 [4, 512, 128, 512], P('cores', None, 'mode'), may hold values from -0.25 to 0.25
- y_cores: bfloat16 [4, 256, 128, 256], P('cores', None, 'mode'), may hold values from -40 to 40
- left_boundary: bfloat16 [256, 512], replicated, may hold values from -6 to 6
- right_boundary: bfloat16 [256, 512], replicated, may hold values from -6 to 6
Outputs:
- projected: bfloat16 [4, 256, 128, 256], P('cores', None, 'mode')
All inputs are finite; a program needn't handle non-finite values.
Results may differ from a plain program's by a relative error of at most 0.014.
Values may be sent and summed in bfloat16 or wider, within the bound.
A program may use at most 128 MiB of HBM per device.

v0:
```python
import functools
import math

import jax
import jax.numpy as jnp
from jax import lax
from jax.experimental import pallas as pl
from jax.experimental.pallas import tpu as pltpu
from jax.sharding import PartitionSpec as P

epsilon = 1e-06
f32 = jnp.float32
bf16 = jnp.bfloat16
NN = (((1,), (0,)), ((), ()))
NT = (((1,), (1,)), ((), ()))
TN = (((0,), (0,)), ((), ()))


def dot(a, b, dims):
    return lax.dot_general(a, b, dims, preferred_element_type=f32)


def kernel(groups, chips, x_hbm, y_hbm, lb, rb, out_hbm, xv, yv, keep, outv, env, acc,
           pair_out, pair_in, stage, parts, x_sem, y_sem, o_sem, pair_sem, part_send, part_recv,
           gather_send, gather_recv, relay_send, relay_recv):
    g = lax.axis_index("cores")
    m = lax.axis_index("mode")
    chip = m // 2
    core = lax.rem(m, 2)
    partner = chip * 2 + (1 - core)
    points = xv.shape[0]
    rank_y, rank_x = lb.shape
    half = rank_y // 2
    row_cuts = min(chips, half // 16)
    col_cuts = chips // row_cuts
    rows, cols = half // row_cuts, rank_x // col_cuts
    norm = 1.0 / math.sqrt(rank_x)

    def x_load(i):
        return pltpu.make_async_copy(x_hbm.at[i], xv.at[i], x_sem.at[i])

    def y_load(i):
        return pltpu.make_async_copy(y_hbm.at[i], yv.at[i], y_sem.at[i])

    def out_store(i):
        return pltpu.make_async_copy(outv.at[i], out_hbm.at[i], o_sem.at[i])

    @pl.loop(0, points)
    def _(i):
        x_load(i).start()
        y_load(i).start()

    barrier = pltpu.get_barrier_semaphore()

    def greet(group, index):
        pl.semaphore_signal(barrier, inc=1, device_id=(group, index), device_id_type=pl.DeviceIdType.MESH)

    greet(g, partner)
    for step in range(1, chips):
        greet(g, lax.rem(chip + step, chips) * 2 + core)

    @pl.when(g > 0)
    def _():
        for j in range(chips):
            greet(g - 1, j * 2 + core)

    @pl.when(g < groups - 1)
    def _():
        for j in range(chips):
            greet(g + 1, j * 2 + core)

    sides = jnp.where(g > 0, 1, 0) + jnp.where(g < groups - 1, 1, 0)
    pl.semaphore_wait(barrier, chips * (1 + sides))

    def remote(src, dst, send, recv, group, index):
        return pltpu.make_async_remote_copy(
            src_ref=src, dst_ref=dst, send_sem=send, recv_sem=recv,
            device_id=(group, index), device_id_type=pl.DeviceIdType.MESH,
        )

    def place(j, base):
        if col_cuts == 1:
            return pl.ds(pl.multiple_of(base + j * rows, rows), rows), pl.ds(0, cols)
        return (
            pl.ds(pl.multiple_of(base + (j // col_cuts) * rows, rows), rows),
            pl.ds(pl.multiple_of(lax.rem(j, col_cuts) * cols, cols), cols),
        )

    def produce(d, scale, store, first):
        acc[...] = jnp.zeros_like(acc)

        @pl.loop(0, points)
        def _(i):
            if first:
                x_load(i).wait()
                y_load(i).wait()
            value = (dot(env[d], xv[i], NT if d else NN) * scale).astype(bf16)
            if store:
                keep[i] = value
            acc[...] += dot(yv[i], value, NN if d else TN)

    def part_copy(d, j, group):
        at = place(j, 0)
        return remote(stage.at[d].at[at[0], at[1]], parts.at[d].at[chip], part_send.at[d, j],
                      part_recv.at[d, chip], group, j * 2 + core)

    def pair_copy(d):
        return remote(pair_out.at[d], pair_in.at[d], pair_sem.at[d, 0], pair_sem.at[d, 1], g, partner)

    def dispatch(d, group):
        other = pl.ds(pl.multiple_of((1 - core) * half, half), half)
        own = pl.ds(pl.multiple_of(core * half, half), half)
        pair_out[d] = acc[other, :].astype(bf16)
        copy = pair_copy(d)
        copy.start()
        copy.wait()
        stage[d] = (acc[own, :] + pair_in[d].astype(f32)).astype(bf16)
        for j in range(chips):
            part_copy(d, j, group).start()

    def finish(d, group):
        for j in range(chips):
            part_copy(d, j, group).wait_send()

    def gather_copy(d, owner, target):
        at = place(owner, core * half)
        block = env.at[d].at[at[0], at[1]]
        return remote(block, block, gather_send.at[d, target], gather_recv.at[d, owner], g, target * 2 + core)

    def relay_copy(d, owner, side):
        at = place(owner, side * half)
        block = env.at[d].at[at[0], at[1]]
        return remote(block, block, relay_send.at[d, owner], relay_recv.at[d, owner], g, partner)

    def collect(d, group):
        total = jnp.zeros((rows, cols), f32)
        for j in range(chips):
            at = place(j, 0)
            remote(stage.at[d].at[at[0], at[1]], parts.at[d].at[j], part_send.at[d, j],
                   part_recv.at[d, j], group, j * 2 + core).wait_recv()
            total = total + parts[d, j].astype(f32)
        at = place(chip, core * half)
        env[d, at[0], at[1]] = total.astype(bf16)
        for step in range(1, chips):
            gather_copy(d, chip, lax.rem(chip + step, chips)).start()
        relay_copy(d, chip, core).start()
        for step in range(1, chips):
            owner = lax.rem(chip + step, chips)
            gather_copy(d, owner, owner).wait_recv()
            relay_copy(d, owner, core).start()
        for j in range(chips):
            relay_copy(d, j, 1 - core).wait_recv()
        for step in range(1, chips):
            gather_copy(d, chip, lax.rem(chip + step, chips)).wait_send()
        for j in range(chips):
            relay_copy(d, j, core).wait_send()

    def level(d):
        values = env[d].astype(f32)
        return lax.rsqrt(jnp.mean(values * values) + epsilon)

    def project(d, scale):
        factor = scale * norm

        @pl.loop(0, points)
        def _(i):
            if d:
                value = dot(keep[i], env[1], NT)
            else:
                value = dot(env[0], keep[i], NT)
            outv[i] = (value * factor).astype(bf16)
            out_store(i).start()

        @pl.loop(0, points)
        def _(i):
            out_store(i).wait()

    def run(first, boundary, edge, ahead, far):
        second = 1 - first
        behind = g - (ahead - g)

        @pl.when(g == edge)
        def _():
            env[first] = boundary[...]

        @pl.when(g != edge)
        def _():
            collect(first, behind)

        scale = jnp.where(g == edge, 1.0, level(first))
        produce(first, scale, True, True)
        dispatch(first, ahead)
        finish(first, ahead)
        collect(second, ahead)
        scale = level(second)

        @pl.when(g != edge)
        def _():
            produce(second, scale, False, False)
            dispatch(second, behind)

        project(second, scale)

        @pl.when(g != edge)
        def _():
            finish(second, behind)

    @pl.when(2 * g < groups)
    def _():
        run(0, lb, 0, g + 1, None)

    @pl.when(2 * g >= groups)
    def _():
        run(1, rb, groups - 1, g - 1, None)


def body(groups, members, x_cores, y_cores, left_boundary, right_boundary):
    rank_y, rank_x = left_boundary.shape
    points = x_cores.shape[2]
    chips = members // 2
    half = rank_y // 2
    row_cuts = min(chips, half // 16)
    col_cuts = chips // row_cuts
    rows, cols = half // row_cuts, rank_x // col_cuts
    x = jnp.transpose(x_cores[0], (1, 0, 2))
    y = jnp.transpose(y_cores[0], (1, 0, 2))
    dma = pltpu.SemaphoreType.DMA
    vmem = pl.BlockSpec(memory_space=pltpu.VMEM)
    anywhere = pl.BlockSpec(memory_space=pl.ANY)
    out = pl.pallas_call(
        functools.partial(kernel, groups, chips),
        out_shape=jax.ShapeDtypeStruct((points, rank_y, rank_y), bf16),
        in_specs=[anywhere, anywhere, vmem, vmem],
        out_specs=anywhere,
        scratch_shapes=[
            pltpu.VMEM((points, rank_x, rank_x), bf16),
            pltpu.VMEM((points, rank_y, rank_y), bf16),
            pltpu.VMEM((points, rank_y, rank_x), bf16),
            pltpu.VMEM((points, rank_y, rank_y), bf16),
            pltpu.VMEM((2, rank_y, rank_x), bf16),
            pltpu.VMEM((rank_y, rank_x), f32),
            pltpu.VMEM((2, half, rank_x), bf16),
            pltpu.VMEM((2, half, rank_x), bf16),
            pltpu.VMEM((2, half, rank_x), bf16),
            pltpu.VMEM((2, chips, rows, cols), bf16),
            dma((points,)), dma((points,)), dma((points,)), dma((2, 2)),
            dma((2, chips)), dma((2, chips)), dma((2, chips)), dma((2, chips)), dma((2, chips)), dma((2, chips)),
        ],
        compiler_params=pltpu.CompilerParams(
            collective_id=0, has_side_effects=True, vmem_limit_bytes=48 * 1024 * 1024
        ),
    )(x, y, left_boundary, right_boundary)
    return jnp.transpose(out, (1, 0, 2))[None]


def solution(mesh):
    in_specs = (P("cores", None, "mode", None), P("cores", None, "mode", None), P(), P())
    out_specs = P("cores", None, "mode", None)
    fn = functools.partial(body, mesh.shape["cores"], mesh.shape["mode"])
    return jax.shard_map(fn, mesh=mesh, in_specs=in_specs, out_specs=out_specs, check_vma=False)
```

profile of v0, /device:TPU:1, one launch (start us, length us, event | category | flops | bytes accessed | tf_op | source)
XLA Modules:
  0.0 94.7 jit_solution(2170125406472577291)
XLA Ops:
  0.0 2.3 %copy.11 = bf16[1,256,16,256]{3,1,2,0:T(8,128)(2,1)S(1)} copy(bf16[1,256,16,256]{3,2,1,0:T(8,128)(2,1)} %param.5) | data formatting | bytes 4194304 | tf_op args[1]
  2.3 0.0 copy-start
  2.3 0.0 copy-start.1
  2.3 11.4 %copy.10 = bf16[1,512,16,512]{3,1,2,0:T(8,128)(2,1)} copy(bf16[1,512,16,512]{3,2,1,0:T(8,128)(2,1)} %param.4) | data formatting | bytes 16777216 | tf_op args[0]
  13.7 0.0 copy-done
  13.7 0.0 copy-done.1
  13.7 78.5 %shard_map.46 = bf16[16,256,256]{2,1,0:T(8,128)(2,1)S(1)} custom-call(bf16[16,512,512]{2,1,0:T(8,128)(2,1)} %bitcast.15, bf16[16,256,256]{2,1,0:T(8,128)(2,1)S(1)} %bitcast.14, bf16[256,512]{1,0:T(8,128)(2,1)S(1)} %copy-done, bf16[256,512]{1,0:T(8,128)(2,1)S(1)} %copy-done.1), custom_call_target="tpu_custom_call" | custom-call | tf_op jit(solution)/shard_map/pallas_call | solution.py:230
  92.3 2.5 %copy.7 = bf16[1,256,16,256]{3,2,1,0:T(8,128)(2,1)} copy(bf16[1,256,16,256]{3,1,2,0:T(8,128)(2,1)S(1)} %bitcast.13) | data formatting | bytes 4194304 | tf_op jit(solution)/shard_map/broadcast_in_dim | solution.py:253
Async XLA Ops:
  2.3 11.4 %copy-start = (bf16[256,512]{1,0:T(8,128)(2,1)S(1)}, bf16[256,512]{1,0:T(8,128)(2,1)}, u32[]{:S(2)}) copy-start(bf16[256,512]{1,0:T(8,128)(2,1)} %lb.1) | copy-start | bytes 786436
  2.3 11.4 %copy-start.1 = (bf16[256,512]{1,0:T(8,128)(2,1)S(1)}, bf16[256,512]{1,0:T(8,128)(2,1)}, u32[]{:S(2)}) copy-start(bf16[256,512]{1,0:T(8,128)(2,1)} %rb.1) | copy-start | bytes 786436
where the time goes:
time: 95 us; the launch traced here: 94.7 us
  Pallas kernels  78.5 us (83%)
  local copies, waits for them, and re-layouts  16.2 us (17%)
    pallas_call x1, Pallas kernels, body(): pl.pallas_call(functools.partial(kernel, groups, chips), out_shape=jax.Sh...  78.5 us
    unnamed x6, local copies, waits for them, and re-layouts  13.7 us
    broadcast_in_dim x1, local copies, waits for them, and re-layouts, body(): return jnp.transpose(out, (1, 0, 2))[None]  2.5 us

commit v1 on v0

v1 whole, which is shorter than its diff:
```python
import functools
import math

import jax
import jax.numpy as jnp
from jax import lax
from jax.experimental import pallas as pl
from jax.experimental.pallas import tpu as pltpu
from jax.sharding import PartitionSpec as P

epsilon = 1e-06
f32 = jnp.float32
bf16 = jnp.bfloat16
chunk = 64
NN = (((1,), (0,)), ((), ()))
NT = (((1,), (1,)), ((), ()))
TN = (((0,), (0,)), ((), ()))


def dot(a, b, dims):
    return lax.dot_general(a, b, dims, preferred_element_type=f32)


def cuts(chips, rank_y, rank_x):
    half = rank_y // 2
    row_cuts = min(chips, half // 16)
    col_cuts = chips // row_cuts
    splits = 1
    width = rank_x // splits
    return half, splits, width, half // row_cuts, width // col_cuts, col_cuts


def kernel(groups, chips, x_hbm, y_hbm, lb, rb, outv, xin, yin, xv, yv, keep, env, acc,
           pair_out, pair_in, stage, parts, level, x_sem, y_sem, pair_send, pair_recv, part_send, part_recv,
           gather_send, gather_recv, relay_send, relay_recv):
    g = lax.axis_index("cores")
    m = lax.axis_index("mode")
    chip = m // 2
    core = lax.rem(m, 2)
    partner = chip * 2 + (1 - core)
    points = xv.shape[0]
    rank_y, rank_x = lb.shape
    half, splits, width, rows, cols, col_cuts = cuts(chips, rank_y, rank_x)
    batch = math.gcd(points, 8)
    batches = points // batch
    norm = 1.0 / math.sqrt(rank_x)

    def load(source, target, sem, j):
        at = pl.ds(pl.multiple_of(j * chunk, chunk), chunk)
        return pltpu.make_async_copy(source.at[at], target.at[at], sem.at[j])

    for j in range(rank_x // chunk):
        load(x_hbm, xin, x_sem, j).start()
    for j in range(rank_y // chunk):
        load(y_hbm, yin, y_sem, j).start()

    def turn(source, held, target, sem):
        @pl.loop(0, source.shape[0] // chunk)
        def _(j):
            load(source, held, sem, j).wait()
            for r in range(0, chunk, 16):
                at = pl.ds(pl.multiple_of(j * chunk + r, 16), 16)
                for c in range(0, source.shape[2], 128):
                    target[:, at, c:c + 128] = jnp.swapaxes(held[at, :, c:c + 128], 0, 1)

    barrier = pltpu.get_barrier_semaphore()

    def greet(group, index):
        pl.semaphore_signal(barrier, inc=1, device_id=(group, index), device_id_type=pl.DeviceIdType.MESH)

    greet(g, partner)
    for step in range(1, chips):
        greet(g, lax.rem(chip + step, chips) * 2 + core)

    @pl.when(g > 0)
    def _():
        for j in range(chips):
            greet(g - 1, j * 2 + core)

    @pl.when(g < groups - 1)
    def _():
        for j in range(chips):
            greet(g + 1, j * 2 + core)

    turn(x_hbm, xin, xv, x_sem)
    turn(y_hbm, yin, yv, y_sem)
    sides = jnp.where(g > 0, 1, 0) + jnp.where(g < groups - 1, 1, 0)
    pl.semaphore_wait(barrier, chips * (1 + sides))

    def remote(src, dst, send, recv, group, index):
        return pltpu.make_async_remote_copy(
            src_ref=src, dst_ref=dst, send_sem=send, recv_sem=recv,
            device_id=(group, index), device_id_type=pl.DeviceIdType.MESH,
        )

    def place(j, base, side):
        if col_cuts == 1:
            return pl.ds(pl.multiple_of(base + j * rows, rows), rows), pl.ds(side, cols)
        return (
            pl.ds(pl.multiple_of(base + (j // col_cuts) * rows, rows), rows),
            pl.ds(pl.multiple_of(side + lax.rem(j, col_cuts) * cols, cols), cols),
        )

    def produce(d, h, scale, store, lo, hi):
        at = pl.ds(h * width, width)

        @pl.loop(lo, hi)
        def _(k):
            summed = None
            for u in range(batch):
                i = k * batch + u
                if d:
                    value = dot(env[1], xv[i, at, :], NT)
                else:
                    value = dot(env[0], xv[i, :, at], NN)
                value = (value * scale).astype(bf16)
                if store:
                    keep[i, :, at] = value
                term = dot(yv[i], value, NN if d else TN)
                summed = term if summed is None else summed + term
            acc[h] += summed

    def part_copy(d, h, j, slot, group):
        at = place(j, 0, 0)
        return remote(stage.at[d, h].at[at[0], at[1]], parts.at[d, h].at[slot], part_send.at[d, h, j],
                      part_recv.at[d, h, slot], group, j * 2 + core)

    def pair_copy(d, h):
        return remote(pair_out.at[d, h], pair_in.at[d, h], pair_send.at[d, h], pair_recv.at[d, h], g, partner)

    def pair_start(d, h):
        other = pl.ds(pl.multiple_of((1 - core) * half, half), half)
        pair_out[d, h] = acc[h, other, :].astype(bf16)
        pair_copy(d, h).start()

    def part_start(d, h, group):
        own = pl.ds(pl.multiple_of(core * half, half), half)
        pair_copy(d, h).wait_recv()
        stage[d, h] = (acc[h, own, :] + pair_in[d, h].astype(f32)).astype(bf16)
        for j in range(chips):
            part_copy(d, h, j, chip, group).start()

    def advance(d, scale, store, group):
        acc[...] = jnp.zeros_like(acc)
        for h in range(splits):
            if h:
                produce(d, h, scale, store, 0, batches // 2)
                part_start(d, h - 1, group)
                produce(d, h, scale, store, batches // 2, batches)
            else:
                produce(d, h, scale, store, 0, batches)
            pair_start(d, h)
        part_start(d, splits - 1, group)

    def finish(d, group):
        for h in range(splits):
            pair_copy(d, h).wait_send()
            for j in range(chips):
                part_copy(d, h, j, chip, group).wait_send()

    def gather_copy(d, h, owner, target):
        at = place(owner, core * half, h * width)
        block = env.at[d].at[at[0], at[1]]
        return remote(block, block, gather_send.at[d, h, target], gather_recv.at[d, h, owner], g, target * 2 + core)

    def relay_copy(d, h, owner, side):
        at = place(owner, side * half, h * width)
        block = env.at[d].at[at[0], at[1]]
        return remote(block, block, relay_send.at[d, h, owner], relay_recv.at[d, h, owner], g, partner)

    def collect(d, group):
        squares = 0.0
        for h in range(splits):
            total = jnp.zeros((rows, cols), f32)
            for j in range(chips):
                part_copy(d, h, j, j, group).wait_recv()
                total = total + parts[d, h, j].astype(f32)
            at = place(chip, core * half, h * width)
            env[d, at[0], at[1]] = total.astype(bf16)
            for step in range(1, chips):
                gather_copy(d, h, chip, lax.rem(chip + step, chips)).start()
            relay_copy(d, h, chip, core).start()
            for step in range(1, chips):
                owner = lax.rem(chip + step, chips)
                gather_copy(d, h, owner, owner).wait_recv()
                relay_copy(d, h, owner, core).start()
            for j in range(chips):
                relay_copy(d, h, j, 1 - core).wait_recv()
            values = env[d, :, pl.ds(h * width, width)].astype(f32)
            squares = squares + jnp.sum(values * values)
        for h in range(splits):
            for step in range(1, chips):
                gather_copy(d, h, chip, lax.rem(chip + step, chips)).wait_send()
            for j in range(chips):
                relay_copy(d, h, j, core).wait_send()
        return lax.rsqrt(squares / (rank_y * rank_x) + epsilon)

    def project(d, scale):
        factor = scale * norm

        @pl.loop(0, batches)
        def _(k):
            group = pl.ds(k * batch, batch)
            if d:
                value = dot(keep[group].reshape(batch * rank_y, rank_x), env[1], NT) * factor
                outv[group] = value.astype(bf16).reshape(batch, rank_y, rank_y)
            else:
                for u in range(batch):
                    outv[k * batch + u] = (dot(env[0], keep[k * batch + u], NT) * factor).astype(bf16)

    def run(first, boundary, edge, ahead):
        second = 1 - first
        behind = g - (ahead - g)

        @pl.when(g == edge)
        def _():
            env[first] = boundary[...]
            level[0] = 1.0

        @pl.when(g != edge)
        def _():
            level[0] = collect(first, behind)

        advance(first, level[0], True, ahead)
        finish(first, ahead)
        scale = collect(second, ahead)

        @pl.when(g != edge)
        def _():
            advance(second, scale, False, behind)

        project(second, scale)

        @pl.when(g != edge)
        def _():
            finish(second, behind)

    @pl.when(2 * g < groups)
    def _():
        run(0, lb, 0, g + 1)

    @pl.when(2 * g >= groups)
    def _():
        run(1, rb, groups - 1, g - 1)


def body(groups, members, x_cores, y_cores, left_boundary, right_boundary):
    rank_y, rank_x = left_boundary.shape
    points = x_cores.shape[2]
    chips = members // 2
    half, splits, width, rows, cols, col_cuts = cuts(chips, rank_y, rank_x)
    dma = pltpu.SemaphoreType.DMA
    vmem = pl.BlockSpec(memory_space=pltpu.VMEM)
    anywhere = pl.BlockSpec(memory_space=pl.ANY)
    out = pl.pallas_call(
        functools.partial(kernel, groups, chips),
        out_shape=jax.ShapeDtypeStruct((points, rank_y, rank_y), bf16),
        in_specs=[anywhere, anywhere, vmem, vmem],
        out_specs=vmem,
        scratch_shapes=[
            pltpu.VMEM((rank_x, points, rank_x), bf16),
            pltpu.VMEM((rank_y, points, rank_y), bf16),
            pltpu.VMEM((points, rank_x, rank_x), bf16),
            pltpu.VMEM((points, rank_y, rank_y), bf16),
            pltpu.VMEM((points, rank_y, rank_x), bf16),
            pltpu.VMEM((2, rank_y, rank_x), bf16),
            pltpu.VMEM((splits, rank_y, width), f32),
            pltpu.VMEM((2, splits, half, width), bf16),
            pltpu.VMEM((2, splits, half, width), bf16),
            pltpu.VMEM((2, splits, half, width), bf16),
            pltpu.VMEM((2, splits, chips, rows, cols), bf16),
            pltpu.SMEM((1,), f32),
            dma((rank_x // chunk,)), dma((rank_y // chunk,)), dma((2, splits)), dma((2, splits)),
            dma((2, splits, chips)), dma((2, splits, chips)), dma((2, splits, chips)),
            dma((2, splits, chips)), dma((2, splits, chips)), dma((2, splits, chips)),
        ],
        compiler_params=pltpu.CompilerParams(
            collective_id=0, has_side_effects=True, vmem_limit_bytes=48 * 1024 * 1024
        ),
    )(x_cores[0], y_cores[0], left_boundary, right_boundary)
    return jnp.transpose(out, (1, 0, 2))[None]


def solution(mesh):
    in_specs = (P("cores", None, "mode", None), P("cores", None, "mode", None), P(), P())
    out_specs = P("cores", None, "mode", None)
    fn = functools.partial(body, mesh.shape["cores"], mesh.shape["mode"])
    return jax.shard_map(fn, mesh=mesh, in_specs=in_specs, out_specs=out_specs, check_vma=False)
```

time: 95 us -> 69.2 us (0.73)
  Pallas kernels: 78.5 us -> 63 us
  local copies, waits for them, and re-layouts: 16.2 us -> 5.98 us
    pallas_call x1, Pallas kernels: 78.5 us -> 63 us  [body(): pl.pallas_call(functools.partial(kernel, groups, chips), out_shape=jax.Sh...]
    unnamed x6, local copies, waits for them, and re-layouts: 13.7 us -> 3.49 us
where the time goes in v1:
time: 69.2 us; the launch traced here: 69 us
  Pallas kernels  63 us (91%)
  local copies, waits for them, and re-layouts  5.98 us (9%)
    pallas_call x1, Pallas kernels, body(): pl.pallas_call(functools.partial(kernel, groups, chips), out_shape=jax.Sh...  63 us
    unnamed x6, local copies, waits for them, and re-layouts  3.49 us
    broadcast_in_dim x1, local copies, waits for them, and re-layouts, body(): return jnp.transpose(out, (1, 0, 2))[None]  2.5 us

profile of v1, /device:TPU:1, one launch (start us, length us, event | category | flops | bytes accessed | tf_op | source)
XLA Modules:
  0.0 69.0 jit_solution(9855841502756895443)
XLA Ops:
  0.0 0.0 copy-start
  0.0 1.6 %copy-done = bf16[1,256,16,256]{3,2,1,0:T(8,128)(2,1)S(1)} copy-done((bf16[1,256,16,256]{3,2,1,0:T(8,128)(2,1)S(1)}, bf16[1,256,16,256]{3,2,1,0:T(8,128)(2,1)}, u32[]{:S(2)}) %copy-start) | copy-done | bytes 2097176
  1.6 0.0 copy-start.1
  1.6 0.9 %copy-done.1 = bf16[256,512]{1,0:T(8,128)(2,1)S(1)} copy-done((bf16[256,512]{1,0:T(8,128)(2,1)S(1)}, bf16[256,512]{1,0:T(8,128)(2,1)}, u32[]{:S(2)}) %copy-start.1) | copy-done | bytes 262168
  2.5 0.0 copy-start.2
  2.5 0.9 %copy-done.2 = bf16[256,512]{1,0:T(8,128)(2,1)S(1)} copy-done((bf16[256,512]{1,0:T(8,128)(2,1)S(1)}, bf16[256,512]{1,0:T(8,128)(2,1)}, u32[]{:S(2)}) %copy-start.2) | copy-done | bytes 262168
  3.5 63.0 %shard_map.46 = bf16[16,256,256]{2,1,0:T(8,128)(2,1)S(1)} custom-call(bf16[512,16,512]{2,1,0:T(8,128)(2,1)} %bitcast.7, bf16[256,16,256]{2,1,0:T(8,128)(2,1)S(1)} %bitcast.6, bf16[256,512]{1,0:T(8,128)(2,1)S(1)} %copy-done.1, bf16[256,512]{1,0:T(8,128)(2,1)S(1)} %copy-done.2), custom_call_target="tpu_custom_call" | custom-call | tf_op jit(solution)/shard_map/pallas_call | solution.py:255
  66.5 2.5 %copy.5 = bf16[1,256,16,256]{3,2,1,0:T(8,128)(2,1)} copy(bf16[1,256,16,256]{3,1,2,0:T(8,128)(2,1)S(1)} %bitcast.5) | data formatting | bytes 4194304 | tf_op jit(solution)/shard_map/broadcast_in_dim | solution.py:281
Async XLA Ops:
  0.0 1.6 %copy-start = (bf16[1,256,16,256]{3,2,1,0:T(8,128)(2,1)S(1)}, bf16[1,256,16,256]{3,2,1,0:T(8,128)(2,1)}, u32[]{:S(2)}) copy-start(bf16[1,256,16,256]{3,2,1,0:T(8,128)(2,1)} %param.5) | copy-start | bytes 6291460
  1.6 0.9 %copy-start.1 = (bf16[256,512]{1,0:T(8,128)(2,1)S(1)}, bf16[256,512]{1,0:T(8,128)(2,1)}, u32[]{:S(2)}) copy-start(bf16[256,512]{1,0:T(8,128)(2,1)} %lb.1) | copy-start | bytes 786436
  2.5 0.9 %copy-start.2 = (bf16[256,512]{1,0:T(8,128)(2,1)S(1)}, bf16[256,512]{1,0:T(8,128)(2,1)}, u32[]{:S(2)}) copy-start(bf16[256,512]{1,0:T(8,128)(2,1)} %rb.1) | copy-start | bytes 786436

commit v2 on v1

--- a/solution.py
+++ b/solution.py
@@ -25,13 +25,13 @@
     half = rank_y // 2
     row_cuts = min(chips, half // 16)
     col_cuts = chips // row_cuts
-    splits = 1
+    splits = 2 if rank_x // 2 // col_cuts >= 128 else 1
     width = rank_x // splits
     return half, splits, width, half // row_cuts, width // col_cuts, col_cuts
 
 
-def kernel(groups, chips, x_hbm, y_hbm, lb, rb, outv, xin, yin, xv, yv, keep, env, acc,
-           pair_out, pair_in, stage, parts, level, x_sem, y_sem, pair_send, pair_recv, part_send, part_recv,
+def kernel(groups, chips, x_hbm, y_hbm, lb, rb, out_hbm, outv, xin, yin, xv, yv, keep, env, acc,
+           pair_out, pair_in, stage, parts, level, x_sem, y_sem, b_sem, o_sem, pair_send, pair_recv, part_send, part_recv,
            gather_send, gather_recv, relay_send, relay_recv):
     g = lax.axis_index("cores")
     m = lax.axis_index("mode")
@@ -54,6 +54,17 @@
     for j in range(rank_y // chunk):
         load(y_hbm, yin, y_sem, j).start()
 
+    def bound(d):
+        return pltpu.make_async_copy(rb if d else lb, env.at[d], b_sem)
+
+    @pl.when(g == 0)
+    def _():
+        bound(0).start()
+
+    @pl.when(g == groups - 1)
+    def _():
+        bound(1).start()
+
     def turn(source, held, target, sem):
         @pl.loop(0, source.shape[0] // chunk)
         def _(j):
@@ -101,24 +112,21 @@
             pl.ds(pl.multiple_of(side + lax.rem(j, col_cuts) * cols, cols), cols),
         )
 
-    def produce(d, h, scale, store, lo, hi):
-        at = pl.ds(h * width, width)
-
-        @pl.loop(lo, hi)
+    def produce(d, scale, store):
+        acc[...] = jnp.zeros_like(acc)
+
+        @pl.loop(0, batches)
         def _(k):
             summed = None
             for u in range(batch):
                 i = k * batch + u
-                if d:
-                    value = dot(env[1], xv[i, at, :], NT)
-                else:
-                    value = dot(env[0], xv[i, :, at], NN)
-                value = (value * scale).astype(bf16)
+                value = (dot(env[d], xv[i], NT if d else NN) * scale).astype(bf16)
                 if store:
-                    keep[i, :, at] = value
+                    keep[i] = value
                 term = dot(yv[i], value, NN if d else TN)
                 summed = term if summed is None else summed + term
-            acc[h] += summed
+            for h in range(splits):
+                acc[h] += summed[:, h * width:(h + 1) * width]
 
     def part_copy(d, h, j, slot, group):
         at = place(j, 0, 0)
@@ -141,16 +149,11 @@
             part_copy(d, h, j, chip, group).start()
 
     def advance(d, scale, store, group):
-        acc[...] = jnp.zeros_like(acc)
-        for h in range(splits):
-            if h:
-                produce(d, h, scale, store, 0, batches // 2)
-                part_start(d, h - 1, group)
-                produce(d, h, scale, store, batches // 2, batches)
-            else:
-                produce(d, h, scale, store, 0, batches)
+        produce(d, scale, store)
+        for h in range(splits):
             pair_start(d, h)
-        part_start(d, splits - 1, group)
+        for h in range(splits):
+            part_start(d, h, group)
 
     def finish(d, group):
         for h in range(splits):
@@ -169,31 +172,36 @@
         return remote(block, block, relay_send.at[d, h, owner], relay_recv.at[d, h, owner], g, partner)
 
     def collect(d, group):
-        squares = 0.0
+        others = [lax.rem(chip + step, chips) for step in range(1, chips)]
         for h in range(splits):
             total = jnp.zeros((rows, cols), f32)
             for j in range(chips):
-                part_copy(d, h, j, j, group).wait_recv()
+                part_copy(d, h, 0, j, group).wait_recv()
                 total = total + parts[d, h, j].astype(f32)
             at = place(chip, core * half, h * width)
             env[d, at[0], at[1]] = total.astype(bf16)
-            for step in range(1, chips):
-                gather_copy(d, h, chip, lax.rem(chip + step, chips)).start()
+            for target in others:
+                gather_copy(d, h, chip, target).start()
             relay_copy(d, h, chip, core).start()
-            for step in range(1, chips):
-                owner = lax.rem(chip + step, chips)
-                gather_copy(d, h, owner, owner).wait_recv()
+        for h in range(splits):
+            for owner in others:
+                gather_copy(d, h, owner, chip).wait_recv()
                 relay_copy(d, h, owner, core).start()
+        squares = 0.0
+        for h in range(splits):
             for j in range(chips):
                 relay_copy(d, h, j, 1 - core).wait_recv()
             values = env[d, :, pl.ds(h * width, width)].astype(f32)
             squares = squares + jnp.sum(values * values)
         for h in range(splits):
-            for step in range(1, chips):
-                gather_copy(d, h, chip, lax.rem(chip + step, chips)).wait_send()
+            for target in others:
+                gather_copy(d, h, chip, target).wait_send()
             for j in range(chips):
                 relay_copy(d, h, j, core).wait_send()
         return lax.rsqrt(squares / (rank_y * rank_x) + epsilon)
+
+    def out_store(i):
+        return pltpu.make_async_copy(outv.at[i], out_hbm.at[i], o_sem.at[i])
 
     def project(d, scale):
         factor = scale * norm
@@ -207,14 +215,20 @@
             else:
                 for u in range(batch):
                     outv[k * batch + u] = (dot(env[0], keep[k * batch + u], NT) * factor).astype(bf16)
-
-    def run(first, boundary, edge, ahead):
+            for u in range(batch):
+                out_store(k * batch + u).start()
+
+        @pl.loop(0, points)
+        def _(i):
+            out_store(i).wait()
+
+    def run(first, edge, ahead):
         second = 1 - first
         behind = g - (ahead - g)
 
         @pl.when(g == edge)
         def _():
-            env[first] = boundary[...]
+            bound(first).wait()
             level[0] = 1.0
 
         @pl.when(g != edge)
@@ -237,11 +251,11 @@
 
     @pl.when(2 * g < groups)
     def _():
-        run(0, lb, 0, g + 1)
+        run(0, 0, g + 1)
 
     @pl.when(2 * g >= groups)
     def _():
-        run(1, rb, groups - 1, g - 1)
+        run(1, groups - 1, g - 1)
 
 
 def body(groups, members, x_cores, y_cores, left_boundary, right_boundary):
@@ -250,14 +264,14 @@
     chips = members // 2
     half, splits, width, rows, cols, col_cuts = cuts(chips, rank_y, rank_x)
     dma = pltpu.SemaphoreType.DMA
-    vmem = pl.BlockSpec(memory_space=pltpu.VMEM)
-    anywhere = pl.BlockSpec(memory_space=pl.ANY)
+    anywhere = pl.BlockSpec(memory_space=pltpu.HBM)
     out = pl.pallas_call(
         functools.partial(kernel, groups, chips),
         out_shape=jax.ShapeDtypeStruct((points, rank_y, rank_y), bf16),
-        in_specs=[anywhere, anywhere, vmem, vmem],
-        out_specs=vmem,
+        in_specs=[anywhere] * 4,
+        out_specs=anywhere,
         scratch_shapes=[
+            pltpu.VMEM((points, rank_y, rank_y), bf16),
             pltpu.VMEM((rank_x, points, rank_x), bf16),
             pltpu.VMEM((rank_y, points, rank_y), bf16),
             pltpu.VMEM((points, rank_x, rank_x), bf16),
@@ -270,12 +284,12 @@
             pltpu.VMEM((2, splits, half, width), bf16),
             pltpu.VMEM((2, splits, chips, rows, cols), bf16),
             pltpu.SMEM((1,), f32),
-            dma((rank_x // chunk,)), dma((rank_y // chunk,)), dma((2, splits)), dma((2, splits)),
+            dma((rank_x // chunk,)), dma((rank_y // chunk,)), dma, dma((points,)), dma((2, splits)), dma((2, splits)),
             dma((2, splits, chips)), dma((2, splits, chips)), dma((2, splits, chips)),
             dma((2, splits, chips)), dma((2, splits, chips)), dma((2, splits, chips)),
         ],
         compiler_params=pltpu.CompilerParams(
-            collective_id=0, has_side_effects=True, vmem_limit_bytes=48 * 1024 * 1024
+            collective_id=0, has_side_effects=True, vmem_limit_bytes=67043328
         ),
     )(x_cores[0], y_cores[0], left_boundary, right_boundary)
     return jnp.transpose(out, (1, 0, 2))[None]

time: 69.2 us -> 67.3 us (0.973)
  local copies, waits for them, and re-layouts: 5.98 us -> 4.08 us
    unnamed x6 -> x0, local copies, waits for them, and re-layouts: 3.49 us -> none
    broadcast_in_dim x1, local copies, waits for them, and re-layouts: 2.5 us -> 4.08 us  [body(): return jnp.transpose(out, (1, 0, 2))[None]]
where the time goes in v2:
time: 67.3 us; the launch traced here: 67.1 us
  Pallas kernels  63 us (94%)
  local copies, waits for them, and re-layouts  4.08 us (6%)
    pallas_call x1, Pallas kernels, body(): pl.pallas_call(functools.partial(kernel, groups, chips), out_shape=jax.Sh...  63 us
    broadcast_in_dim x1, local copies, waits for them, and re-layouts, body(): return jnp.transpose(out, (1, 0, 2))[None]  4.08 us

profile of v2, /device:TPU:1, one launch (start us, length us, event | category | flops | bytes accessed | tf_op | source)
XLA Modules:
  0.0 67.1 jit_solution(4359162588986042350)
XLA Ops:
  0.0 63.0 %shard_map.46 = bf16[16,256,256]{2,1,0:T(8,128)(2,1)} custom-call(bf16[512,16,512]{2,1,0:T(8,128)(2,1)} %bitcast.6, bf16[256,16,256]{2,1,0:T(8,128)(2,1)} %bitcast.7, bf16[256,512]{1,0:T(8,128)(2,1)} %lb.1, bf16[256,512]{1,0:T(8,128)(2,1)} %rb.1), custom_call_target="tpu_custom_call" | custom-call | tf_op jit(solution)/shard_map/pallas_call | solution.py:268
  63.0 4.1 %copy.5 = bf16[1,256,16,256]{3,2,1,0:T(8,128)(2,1)} copy(bf16[1,256,16,256]{3,1,2,0:T(8,128)(2,1)} %bitcast.5) | data formatting | bytes 4194304 | tf_op jit(solution)/shard_map/broadcast_in_dim | solution.py:295
